TPU v7x, 32 devices: a whole 2x2x4 slice. The times are simulated.
32 devices in a mesh: pb: 8 (over y, x, core), pa: 4 (over z).
Axes of the slice: x: 2, y: 2, z: 4, core: 2. Of those that a mesh axis runs over, the one named last changes fastest.
Arguments:
- queries: bfloat16 [2048, 128], P('pb'), may hold values from -10.5 to 10.5, as said below
- encoder_outputs: bfloat16 [8, 64, 128, 1024], P('pb', 'pa'), may hold values from -6 to 6
- proj_weight: bfloat16 [1024, 128], replicated, may hold values from -0.1875 to 0.1875
- bm25_rank: int32 [64, 4, 64], P('pb', 'pa'), may hold values from 0 to 199
- dense_rank: int32 [64, 4, 64], P('pb', 'pa'), may hold values from 0 to 199
- custodian_document_index: int32 [8, 64], P('pb', 'pa'), may hold values from -1 to 31, as said below
Outputs:
- query_grad: float32 [2048, 128], P(('pb', 'pa'))
- encoder_output_derivative: bfloat16 [8, 64, 128, 1024], P('pb', 'pa')
Inputs may be any that keep to these rules, and one draw needn't show every extreme that they name: `queries`: A custom draw: each entry lies between the bounds; rows may differ in scale. `custodian_document_index`: within each row b every number n from 0 to 31 appears exactly once and stands for passage (n // 8, b * 8 + n % 8); all other entries are -1. The owner of columns o * 16 to o * 16 + 15 is index o of pa; an owner holds 0, 8 or 16 passages, and at most 4 with the same n // 8. Some owner is full and some owner holds exactly 4 passages with the same n // 8 in every row.
All inputs are finite; a program needn't handle non-finite values.
Results may differ from a plain program's by a relative error of at most 0.025.
The roundings to bfloat16 on the way count: a program that leaves them out, or rounds other values in their place, can miss the bound.
Values may be sent and summed in bfloat16 or wider, within the bound.
A program may use at most 64 MiB of HBM per device.

v0:
```python
import jax
import jax.numpy as jnp
from jax import lax
from jax.sharding import PartitionSpec as P

DIM = 128
H = 1024
QT = 32
LEN = 128
PD = 8
DEPTH = 100
CAP = 16
tau = 0.05
inv_temp = 20.0
rrf_offset = 60.0
norm_eps = 1e-06


def normalize(hid_rows, weight):
    projected = jnp.dot(hid_rows, weight, preferred_element_type=jnp.float32)
    scaling = lax.rsqrt(jnp.sum(projected * projected, axis=-1, keepdims=True) + norm_eps)
    return (projected * scaling, scaling)


def joined_target(bm25_rank, dense_rank):
    first = jnp.where(
        bm25_rank < DEPTH, rrf_offset / (rrf_offset + bm25_rank.astype(jnp.float32)), 0.0
    )
    second = jnp.where(
        dense_rank < DEPTH, rrf_offset / (rrf_offset + dense_rank.astype(jnp.float32)), 0.0
    )
    return first + second


def routing(slot_ids, width_pa, sendable):
    filled = slot_ids >= 0
    destination = jnp.where(filled, slot_ids // PD, -1)
    positions = jnp.arange(CAP, dtype=jnp.int32)
    earlier = (destination[None, :] == destination[:, None]) & (
        positions[None, :] < positions[:, None]
    )
    rank_in = jnp.sum(earlier.astype(jnp.int32), axis=1)
    target_at = jnp.where(filled, destination * sendable + rank_in, width_pa * sendable)
    flat_index = jnp.arange(width_pa * sendable, dtype=jnp.int32)
    matches = target_at[None, :] == flat_index[:, None]
    present = jnp.any(matches, axis=1)
    source = jnp.sum(jnp.where(matches, positions[None, :], 0), axis=1)
    labels = jnp.sum(jnp.where(matches, slot_ids[None, :] % PD, 0), axis=1)
    labels = jnp.where(present, labels, -1)
    return (filled, target_at, source, present, labels)


def pick_rows(table, index_list, keep):
    picked = jnp.take(table, jnp.clip(index_list, 0, table.shape[0] - 1), axis=0)
    keep_shape = keep.reshape(keep.shape + (1,) * (picked.ndim - 1))
    return jnp.where(keep_shape, picked, jnp.zeros((), picked.dtype))


def arrival_index(labels):
    wanted = jnp.arange(PD, dtype=jnp.int32)
    matches = labels[None, :] == wanted[:, None]
    slot_numbers = jnp.arange(labels.shape[0], dtype=jnp.int32)
    return jnp.sum(jnp.where(matches, slot_numbers[None, :], 0), axis=1)


def similarity(query_rows, key_block):
    shards = key_block.shape[0]
    flat_keys = key_block.reshape(shards * LEN, key_block.shape[-1])
    raw = (
        jnp.einsum("rd,kd->rk", query_rows, flat_keys, preferred_element_type=jnp.float32)
        * inv_temp
    )
    return raw.reshape(query_rows.shape[0], shards, LEN)


def log_total(raw):
    largest = jnp.max(raw, axis=2, keepdims=True)
    return largest[:, :, 0] + jnp.log(jnp.sum(jnp.exp(raw - largest), axis=2))


def on_device(
    queries, encoder_outputs, proj_weight, bm25_rank, dense_rank, custodian_document_index
):
    width_pa = lax.axis_size("pa")
    sendable = (2 * PD + width_pa - 1) // width_pa
    query_rows = queries.shape[0]
    query_count = query_rows // QT
    passages_all = bm25_rank.shape[2]
    zero_index = jnp.int32(0)
    hid_slots = encoder_outputs[0]
    slot_ids = custodian_document_index[0]
    filled, target_at, source, present, labels = routing(slot_ids, width_pa, sendable)
    unit_rows, scaling = normalize(hid_slots.reshape(CAP * LEN, H), proj_weight)
    emb_slots = unit_rows.astype(jnp.bfloat16).reshape(CAP, LEN, DIM)
    outgoing = pick_rows(emb_slots, source, present).reshape(width_pa, sendable, LEN, DIM)
    arrived, arrived_labels = (
        lax.all_to_all(outgoing, "pa", split_axis=0, concat_axis=0, tiled=True),
        lax.all_to_all(
            labels.reshape(width_pa, sendable), "pa", split_axis=0, concat_axis=0, tiled=True
        ),
    )
    arrived_flat = arrived.reshape(width_pa * sendable, LEN, DIM)
    label_flat = arrived_labels.reshape(width_pa * sendable)
    local_emb = jnp.take(arrived_flat, arrival_index(label_flat), axis=0)
    lse_start = jnp.zeros((query_rows, passages_all), jnp.float32)
    forward_start = (lse_start,)
    key_pieces = lax.all_gather(local_emb, "pb", axis=0, tiled=True)
    begin_at = jnp.int32(0)
    shards = key_pieces.shape[0] // PD

    def forward_one_shard(turn, state):
        key_block = lax.dynamic_slice_in_dim(key_pieces, turn * PD, PD, 0)
        sums = log_total(similarity(queries, key_block))
        return lax.dynamic_update_slice(state, sums, (zero_index, turn * PD))

    lse_part = lax.fori_loop(0, shards, forward_one_shard, forward_start[0])
    kept_parts = tuple(
        (
            lax.dynamic_update_slice_in_dim(kept, key_pieces, begin_at, 0)
            for kept in forward_start[1:]
        )
    )
    forward_state = (lse_part,) + kept_parts
    lse_all = forward_state[0]
    score = lse_all.reshape(query_count, QT, passages_all).sum(axis=1) * (tau / QT)
    residual = (score - joined_target(bm25_rank[:, 0, :], dense_rank[:, 0, :])).astype(jnp.bfloat16)
    residual_rows = jnp.repeat(residual, QT, axis=0)
    residual_wide = residual_rows.astype(jnp.float32)
    start_state = (
        jnp.zeros((query_rows, DIM), jnp.float32),
        jnp.zeros((passages_all * LEN, DIM), jnp.float32),
    )
    backward_key_pieces = lax.all_gather(local_emb, "pb", axis=0, tiled=True)
    shards = backward_key_pieces.shape[0] // PD

    def backward_one_shard(turn, state):
        query_acc, emb_acc = state
        offset = turn * PD
        key_block = lax.dynamic_slice_in_dim(backward_key_pieces, turn * PD, PD, 0)
        raw = similarity(queries, key_block)
        log_sums = lax.dynamic_slice_in_dim(lse_all, offset, PD, 1)
        weights = jnp.exp(raw - log_sums[:, :, None])
        residual_cols = lax.dynamic_slice_in_dim(residual_wide, offset, PD, 1)
        coefficient = (
            ((residual_cols / QT)[:, :, None] * weights)
            .astype(jnp.bfloat16)
            .reshape(query_rows, PD * LEN)
        )
        query_acc = query_acc + jnp.dot(
            coefficient, key_block.reshape(PD * LEN, DIM), preferred_element_type=jnp.float32
        )
        emb_part = jnp.einsum("rk,rd->kd", coefficient, queries, preferred_element_type=jnp.float32)
        emb_acc = lax.dynamic_update_slice(emb_acc, emb_part, (offset * LEN, zero_index))
        return (query_acc, emb_acc)

    query_acc, emb_acc = lax.fori_loop(0, shards, backward_one_shard, start_state)
    query_grad = lax.psum_scatter(
        query_acc.astype(jnp.bfloat16), "pa", scatter_dimension=0, tiled=True
    ).astype(jnp.float32)
    emb_grad = lax.psum_scatter(
        emb_acc.astype(jnp.bfloat16), "pb", scatter_dimension=0, tiled=True
    ).reshape(PD, LEN, DIM)
    keep_back = label_flat >= 0
    returning = pick_rows(emb_grad, label_flat, keep_back).reshape(width_pa, sendable, LEN, DIM)
    came_back = lax.all_to_all(returning, "pa", split_axis=0, concat_axis=0, tiled=True).reshape(
        width_pa * sendable, LEN, DIM
    )
    slot_grad = pick_rows(came_back, target_at, filled).astype(jnp.float32).reshape(CAP * LEN, DIM)
    inner = jnp.sum(unit_rows * slot_grad, axis=-1, keepdims=True)
    slot_proj_grad = ((slot_grad - unit_rows * inner) * scaling).astype(jnp.bfloat16)
    hid_grad = jnp.einsum(
        "rd,hd->rh", slot_proj_grad, proj_weight, preferred_element_type=jnp.float32
    )
    encoder_output_derivative = hid_grad.astype(jnp.bfloat16).reshape(1, CAP, LEN, H)
    return (query_grad, encoder_output_derivative)


def solution(mesh):
    return jax.shard_map(
        on_device,
        mesh=mesh,
        in_specs=(
            P("pb", None),
            P("pb", "pa", None, None),
            P(),
            P("pb", "pa", None),
            P("pb", "pa", None),
            P("pb", "pa"),
        ),
        out_specs=(P(("pb", "pa"), None), P("pb", "pa", None, None)),
        check_vma=False,
    )
```

profile of v0, /device:TPU:0, one launch (start us, length us, event | category | flops | bytes accessed | tf_op | source)
XLA Modules:
  0.0 195.5 jit_solution(11533505428949204612)
XLA Ops:
  7.2 0.7 fusion.34
  7.9 0.7 fusion.22
  8.7 0.7 fusion.18
  9.6 0.7 select_n.172
  10.3 6.3 %all-to-all-start = ((s32[4,1,4]{2,1,0:T(1,128)}), s32[4,1,4]{2,1,0:T(1,128)S(1)}, u32[]{:S(2)}, u32[]{:S(2)}) async-start(s32[4,1,4]{2,1,0:T(1,128)} %bitcast.9), calls=%async_computation | async-start | bytes 4096 | tf_op jit(solution)/shard_map/all_to_all | solution.py:98
  16.7 3.5 %multiply_reduce_fusion = (f32[2048]{0:T(1024)S(1)}, f32[2048,128]{1,0:T(8,128)S(1)}) fusion(bf16[2048,1024]{1,0:T(8,128)(2,1)} %bitcast.128, bf16[1024,128]{1,0:T(8,128)(2,1)S(1)} %copy-done), kind=kOutput, calls=%fused_computation.31 | convolution fusion | flops 537393152 | bytes 5513216 | tf_op jit(solution)/shard_map/dot_general | solution.py:20
  20.2 0.9 copy-done.1
  21.6 0.6 gather_fusion.2
  22.2 0.9 select_select_fusion.1
  23.2 5.1 %all-to-all-start.1 = ((bf16[4,4,128,128]{3,2,1,0:T(8,128)(2,1)}), bf16[4,4,128,128]{3,2,1,0:T(8,128)(2,1)S(1)}, u32[]{:S(2)}, u32[]{:S(2)}) async-start(bf16[4,4,128,128]{3,2,1,0:T(8,128)(2,1)} %bitcast.12), calls=%async_computation.1 | async-start | bytes 1048576 | tf_op jit(solution)/shard_map/all_to_all | solution.py:97
  28.3 0.5 broadcast.369
  28.8 0.7 fusion.23
  29.7 12.5 %all-to-all-done.1 = bf16[4,4,128,128]{3,2,1,0:T(8,128)(2,1)S(1)} async-done(((bf16[4,4,128,128]{3,2,1,0:T(8,128)(2,1)}), bf16[4,4,128,128]{3,2,1,0:T(8,128)(2,1)S(1)}, u32[]{:S(2)}, u32[]{:S(2)}) %all-to-all-start.1) | async-done | bytes 524320 | tf_op jit(solution)/shard_map/all_to_all | solution.py:97
  42.2 0.6 gather_fusion
  42.8 0.8 broadcast_select_fusion
  43.7 26.9 %all-gather.2.cloned.1.call-done = bf16[64,128,128]{2,1,0:T(8,128)(2,1)} async-done(((bf16[8,128,128]{2,1,0:T(8,128)(2,1)}), bf16[64,128,128]{2,1,0:T(8,128)(2,1)}) %all-gather.2.cloned.1.call-update) | async-done | bytes 2097168 | tf_op jit(solution)/shard_map/all_gather | solution.py:133
  70.7 11.9 %while.31 = (s32[]{:T(128)}, f32[256,64]{0,1:T(8,128)S(1)}, bf16[64,128,128]{2,1,0:T(8,128)(2,1)}, bf16[256,128]{1,0:T(8,128)(2,1)S(1)}, s32[]{:T(128)}, /*index=5*/s32[]{:T(128)}, s32[]{:T(128)}, s32[]{:T(128)}) while((s32[]{:T(128)}, f32[256,64]{0,1:T(8,128)S(1)}, bf16[64,128,128]{2,1,0:T(8,128)(2,1)}, bf16[256,128]{1,0:T(8,128)(2,1)S(1)}, ...), condition=%wide.region_9.11_spmd, body=%wide.region_6.10_spmd.sunk | while | flops 68155400 | bytes 2998419 | solution.py:116
  70.7 1.0 constant_dynamic-slice_fusion.5
  72.2 1.0 constant_dynamic-slice_fusion.5
  73.7 1.0 constant_dynamic-slice_fusion.5
  75.1 1.0 constant_dynamic-slice_fusion.5
  76.6 1.0 constant_dynamic-slice_fusion.5
  78.1 1.0 constant_dynamic-slice_fusion.5
  79.6 1.0 constant_dynamic-slice_fusion.5
  81.1 1.0 constant_dynamic-slice_fusion.5
  82.8 1.5 broadcast_in_dim.131
  84.3 27.7 %while.32 = (s32[]{:T(128)}, f32[256,128]{1,0:T(8,128)S(1)}, bf16[8192,128]{1,0:T(8,128)(2,1)}, f32[256,64]{0,1:T(8,128)S(1)}, bf16[64,128,128]{2,1,0:T(8,128)(2...) while((s32[]{:T(128)}, f32[256,128]{1,0:T(8,128)S(1)}, ...), condition=%wide.region_12.14_spmd.clone, body=%wide.region_11.13_spmd.clone.sunk | while | flops 203229184 | bytes 7274743 | solution.py:156
  84.3 1.0 constant_dynamic-slice_fusion.6
  86.0 0.7 fusion.54
  86.7 1.0 convolution_dynamic-update-slice_fusion.2
  87.7 1.0 constant_dynamic-slice_fusion.6
  89.4 0.7 fusion.54
  90.2 1.0 convolution_dynamic-update-slice_fusion.2
  91.2 1.0 constant_dynamic-slice_fusion.6
  92.2 0.4 fusion.53
  92.9 0.7 fusion.54
  93.7 1.0 convolution_dynamic-update-slice_fusion.2
  94.7 1.0 constant_dynamic-slice_fusion.6
  95.7 0.4 fusion.53
  96.4 0.7 fusion.54
  97.1 1.0 convolution_dynamic-update-slice_fusion.2
  98.1 1.0 constant_dynamic-slice_fusion.6
  99.1 0.4 fusion.53
  99.8 0.7 fusion.54
  100.6 1.0 convolution_dynamic-update-slice_fusion.2
  101.6 1.0 constant_dynamic-slice_fusion.6
  103.3 0.7 fusion.54
  104.0 1.0 convolution_dynamic-update-slice_fusion.2
  105.1 1.0 constant_dynamic-slice_fusion.6
  106.8 0.7 fusion.54
  107.5 1.0 convolution_dynamic-update-slice_fusion.2
  108.5 1.0 constant_dynamic-slice_fusion.6
  110.2 0.7 fusion.54
  111.0 1.0 convolution_dynamic-update-slice_fusion.2
  112.2 41.1 %reduce-scatter.5.cloned.1.call-done = bf16[1024,128]{1,0:T(8,128)(2,1)} async-done(((bf16[8192,128]{1,0:T(8,128)(2,1)}), bf16[1024,128]{1,0:T(8,128)(2,1)}) %reduce-scatter.5.cloned.1.call-update) | async-done | bytes 262160 | tf_op jit(solution)/shard_map/reduce_scatter | solution.py:160
  153.2 1.6 gather_fusion.1
  154.9 0.9 select_select_fusion.2
  155.8 4.6 %all-to-all-start.2 = ((bf16[4,4,128,128]{3,2,1,0:T(8,128)(2,1)}), bf16[4,4,128,128]{3,2,1,0:T(8,128)(2,1)S(1)}, u32[]{:S(2)}, u32[]{:S(2)}) async-start(bf16[4,4,128,128]{3,2,1,0:T(8,128)(2,1)} %select_select_fusion.2), calls=%async_computation.4 | async-start | bytes 1048576 | tf_op jit(solution)/shard_map/all_to_all | solution.py:165
  160.4 0.6 convert_element_type.65
  161.2 22.1 %reduce-scatter.3.cloned.1.call-done = bf16[64,128]{1,0:T(8,128)(2,1)} async-done(((bf16[256,128]{1,0:T(8,128)(2,1)}), bf16[64,128]{1,0:T(8,128)(2,1)}) %reduce-scatter.3.cloned.1.call-update) | async-done | bytes 16400 | tf_op jit(solution)/shard_map/reduce_scatter | solution.py:157
  183.3 1.3 convert_element_type.66
  184.6 0.6 gather_fusion.3
  185.4 0.7 fusion.8
  186.1 2.9 %convolution_convert_fusion = bf16[2048,1024]{1,0:T(8,128)(2,1)} fusion(bf16[1024,128]{1,0:T(8,128)(2,1)S(1)} %copy-done, bf16[2048,128]{1,0:T(8,128)(2,1)S(1)} %bitcast.129, f32[2048,128]{1,0:T(8,128)S(1)} %copy-done.2, f32[2048]{0:T(1024)S(1)} %fusion.8, f32[2048]{0:T(1024)S(1)} %add_rsqrt_fusion), kind=kOutput, calls=%fused_computation.25 | convolution fusion | flops 540540928 | bytes 6045696 | tf_op jit(solution)/shard_map/rd,hd->rh/dot_general | solution.py:171
  (96 shorter events, 10.0 us)
Async XLA Ops:
  7.2 9.5 %copy-start = (bf16[1024,128]{1,0:T(8,128)(2,1)S(1)}, bf16[1024,128]{1,0:T(8,128)(2,1)}, u32[]{:S(2)}) copy-start(bf16[1024,128]{1,0:T(8,128)(2,1)} %param.14) | copy-start | bytes 786436
  10.3 12.8 %all-to-all-start = ((s32[4,1,4]{2,1,0:T(1,128)}), s32[4,1,4]{2,1,0:T(1,128)S(1)}, u32[]{:S(2)}, u32[]{:S(2)}) async-start(s32[4,1,4]{2,1,0:T(1,128)} %bitcast.9), calls=%async_computation | async-start | bytes 4096 | tf_op jit(solution)/shard_map/all_to_all | solution.py:98
  20.2 1.0 copy-start.1
  21.5 22.1 %copy-start.4 = (s32[8,1,64]{2,1,0:T(1,128)S(1)}, s32[8,1,64]{2,1,0:T(1,128)}, u32[]{:S(2)}) copy-start(s32[8,1,64]{2,1,0:T(1,128)} %param.15) | copy-start | bytes 6148
  21.5 22.1 %copy-start.5 = (s32[8,1,64]{2,1,0:T(1,128)S(1)}, s32[8,1,64]{2,1,0:T(1,128)}, u32[]{:S(2)}) copy-start(s32[8,1,64]{2,1,0:T(1,128)} %param.16) | copy-start | bytes 6148
  21.5 49.1 %copy-start.3 = (bf16[256,128]{1,0:T(8,128)(2,1)S(1)}, bf16[256,128]{1,0:T(8,128)(2,1)}, u32[]{:S(2)}) copy-start(bf16[256,128]{1,0:T(8,128)(2,1)} %param.12) | copy-start | bytes 196612
  23.2 19.0 %all-to-all-start.1 = ((bf16[4,4,128,128]{3,2,1,0:T(8,128)(2,1)}), bf16[4,4,128,128]{3,2,1,0:T(8,128)(2,1)S(1)}, u32[]{:S(2)}, u32[]{:S(2)}) async-start(bf16[4,4,128,128]{3,2,1,0:T(8,128)(2,1)} %bitcast.12), calls=%async_computation.1 | async-start | bytes 1048576 | tf_op jit(solution)/shard_map/all_to_all | solution.py:97
  28.2 42.4 %all-gather.2.cloned.1.call-start = ((), (), s32[]{:S(2)}) async-start(), calls=%async_computation.5 | async-start | bytes 2359296 | tf_op jit(solution)/shard_map/all_gather | solution.py:133
  43.6 109.6 %reduce-scatter.5.cloned.1.call-start = ((), (), s32[]{:S(2)}) async-start(), calls=%async_computation.7 | async-start | bytes 2359296 | tf_op jit(solution)/shard_map/reduce_scatter | solution.py:160
  112.0 49.1 %copy-start.6 = (s32[1,16]{1,0:T(1,128)S(1)}, s32[1,16]{1,0:T(1,128)}, u32[]{:S(2)}) copy-start(s32[1,16]{1,0:T(1,128)} %param.17) | copy-start | bytes 196
  154.9 30.6 %copy-start.2 = (f32[2048,128]{1,0:T(8,128)S(1)}, f32[2048,128]{1,0:T(8,128)}, u32[]{:S(2)}) copy-start(f32[2048,128]{1,0:T(8,128)} %copy-done.1) | copy-start | bytes 3145732
  155.8 28.8 %all-to-all-start.2 = ((bf16[4,4,128,128]{3,2,1,0:T(8,128)(2,1)}), bf16[4,4,128,128]{3,2,1,0:T(8,128)(2,1)S(1)}, u32[]{:S(2)}, u32[]{:S(2)}) async-start(bf16[4,4,128,128]{3,2,1,0:T(8,128)(2,1)} %select_select_fusion.2), calls=%async_computation.4 | async-start | bytes 1048576 | tf_op jit(solution)/shard_map/all_to_all | solution.py:165
  160.4 22.9 %reduce-scatter.3.cloned.1.call-start = ((), (), s32[]{:S(2)}) async-start(), calls=%async_computation.6 | async-start | bytes 81920 | tf_op jit(solution)/shard_map/reduce_scatter | solution.py:157
Sparse Core Ops, SparseCore 0:
  43.7 26.8 all-gather.1
  112.1 41.0 reduce-scatter.4
  163.4 19.7 reduce-scatter.2
where the time goes:
time: 196 us
  waiting for transfers between devices  103 us (53%)
  matrix products  25.7 us (13%)
  local copies, waits for them, and re-layouts  25.6 us (13%)
  starting transfers between devices  16.1 us (8%)
  between operations  14 us (7%)
  other arithmetic  10.6 us (5%)
    reduce_scatter x1, waiting for transfers between devices, on_device(): lax.psum_scatter(emb_acc.astype(jnp.bfloat16), 'pb', scatter_dimension=0,...  41.1 us
    all_gather x1, waiting for transfers between devices, on_device(): backward_key_pieces = lax.all_gather(local_emb, 'pb', axis=0, tiled=True)  26.9 us
    reduce_scatter x1, waiting for transfers between devices, on_device(): lax.psum_scatter(query_acc.astype(jnp.bfloat16), 'pa', scatter_dimension=...  22.1 us
    all_to_all x1, waiting for transfers between devices, on_device(): lax.all_to_all(outgoing, 'pa', split_axis=0, concat_axis=0, tiled=True)  12.5 us
    dot_general x8, matrix products, backward_one_shard(): jnp.einsum('rk,rd->kd', coefficient, queries, preferred_element_type=jnp....  8.05 us
    dynamic_slice x8, local copies, waits for them, and re-layouts, forward_one_shard(): key_block = lax.dynamic_slice_in_dim(key_pieces, turn * PD, PD, 0)  7.78 us
    dynamic_slice x8, local copies, waits for them, and re-layouts, backward_one_shard(): key_block = lax.dynamic_slice_in_dim(backward_key_pieces, turn * PD, PD, 0)  7.74 us
    all_to_all x1, starting transfers between devices, on_device(): lax.all_to_all(labels.reshape(width_pa, sendable), 'pa', split_axis=0, co...  6.35 us
  transfers between devices with their start and end apart: 6, of which 4 were waited for; matrix products, arithmetic and copies ran while one was open for 5% of the time, Pallas kernels for 0%

commit v1 on v0

--- a/solution.py
+++ b/solution.py
@@ -130,7 +130,12 @@
         jnp.zeros((query_rows, DIM), jnp.float32),
         jnp.zeros((passages_all * LEN, DIM), jnp.float32),
     )
-    backward_key_pieces = lax.all_gather(local_emb, "pb", axis=0, tiled=True)
+    ring = [local_emb]
+    for hop in range(7):
+        ring.append(lax.ppermute(ring[-1], "pb", [(dev, (dev + 1) % 8) for dev in range(8)]))
+    backward_key_pieces = jnp.roll(
+        jnp.concatenate(ring[::-1], axis=0), (lax.axis_index("pb") + 1) * ring[0].shape[0], axis=0
+    )
     shards = backward_key_pieces.shape[0] // PD
 
     def backward_one_shard(turn, state):

time: 196 us -> 221 us (1.13)
  waiting for transfers between devices: 103 us -> 126 us
    ppermute x0 -> x7, waiting for transfers between devices: none -> 51.2 us  [on_device(): lax.ppermute(ring[-1], 'pb', [(dev, (dev + 1) % 8) for dev in range(8)])]
    all_gather x1, waiting for transfers between devices: 26.9 us -> 0.01 us  [on_device(): key_pieces = lax.all_gather(local_emb, 'pb', axis=0, tiled=True)]
  transfers between devices with their start and end apart: 6 -> 13, of which waited for: 4 -> 10; matrix products, arithmetic and copies ran while one was open for 5% -> 5% of each run, Pallas kernels for 0% -> 0%
where the time goes in v1:
time: 221 us; the launch traced here: 220 us
  waiting for transfers between devices  126 us (57%)
  local copies, waits for them, and re-layouts  27.6 us (12%)
  matrix products  25.8 us (12%)
  starting transfers between devices  16.2 us (7%)
  between operations  14.1 us (6%)
  other arithmetic  10.2 us (5%)
    ppermute x7, waiting for transfers between devices, on_device(): lax.ppermute(ring[-1], 'pb', [(dev, (dev + 1) % 8) for dev in range(8)])  51.2 us
    reduce_scatter x1, waiting for transfers between devices, on_device(): lax.psum_scatter(emb_acc.astype(jnp.bfloat16), 'pb', scatter_dimension=0,...  39.8 us
    reduce_scatter x1, waiting for transfers between devices, on_device(): lax.psum_scatter(query_acc.astype(jnp.bfloat16), 'pa', scatter_dimension=...  22 us
    all_to_all x1, waiting for transfers between devices, on_device(): lax.all_to_all(outgoing, 'pa', split_axis=0, concat_axis=0, tiled=True)  12.5 us
    dot_general x8, matrix products, backward_one_shard(): jnp.einsum('rk,rd->kd', coefficient, queries, preferred_element_type=jnp....  8.09 us
    dynamic_slice x8, local copies, waits for them, and re-layouts, forward_one_shard(): key_block = lax.dynamic_slice_in_dim(key_pieces, turn * PD, PD, 0)  7.8 us
    dynamic_slice x8, local copies, waits for them, and re-layouts, backward_one_shard(): key_block = lax.dynamic_slice_in_dim(backward_key_pieces, turn * PD, PD, 0)  7.79 us
    all_to_all x1, starting transfers between devices, on_device(): lax.all_to_all(labels.reshape(width_pa, sendable), 'pa', split_axis=0, co...  6.35 us
  transfers between devices with their start and end apart: 13, of which 10 were waited for; matrix products, arithmetic and copies ran while one was open for 5% of the time, Pallas kernels for 0%

profile of v1, /device:TPU:0, one launch (start us, length us, event | category | flops | bytes accessed | tf_op | source)
XLA Modules:
  0.0 220.5 jit_solution(17515156087065264146)
XLA Ops:
  7.2 0.7 fusion.22
  7.9 0.7 fusion.34
  8.7 0.7 fusion.18
  9.6 0.7 select_n.184
  10.3 6.3 %all-to-all-start = ((s32[4,1,4]{2,1,0:T(1,128)}), s32[4,1,4]{2,1,0:T(1,128)S(1)}, u32[]{:S(2)}, u32[]{:S(2)}) async-start(s32[4,1,4]{2,1,0:T(1,128)} %bitcast.9), calls=%async_computation | async-start | bytes 4096 | tf_op jit(solution)/shard_map/all_to_all | solution.py:98
  16.7 3.5 %multiply_reduce_fusion = (f32[2048]{0:T(1024)S(1)}, f32[2048,128]{1,0:T(8,128)S(1)}) fusion(bf16[2048,1024]{1,0:T(8,128)(2,1)} %bitcast.128, bf16[1024,128]{1,0:T(8,128)(2,1)S(1)} %copy-done), kind=kOutput, calls=%fused_computation.31 | convolution fusion | flops 537393152 | bytes 5513216 | tf_op jit(solution)/shard_map/dot_general | solution.py:20
  20.3 0.9 copy-done.1
  21.6 0.6 gather_fusion.2
  22.2 0.9 select_select_fusion.1
  23.1 5.1 %all-to-all-start.1 = ((bf16[4,4,128,128]{3,2,1,0:T(8,128)(2,1)}), bf16[4,4,128,128]{3,2,1,0:T(8,128)(2,1)S(1)}, u32[]{:S(2)}, u32[]{:S(2)}) async-start(bf16[4,4,128,128]{3,2,1,0:T(8,128)(2,1)} %bitcast.12), calls=%async_computation.1 | async-start | bytes 1048576 | tf_op jit(solution)/shard_map/all_to_all | solution.py:97
  28.8 0.7 fusion.23
  29.7 12.5 %all-to-all-done.1 = bf16[4,4,128,128]{3,2,1,0:T(8,128)(2,1)S(1)} async-done(((bf16[4,4,128,128]{3,2,1,0:T(8,128)(2,1)}), bf16[4,4,128,128]{3,2,1,0:T(8,128)(2,1)S(1)}, u32[]{:S(2)}, u32[]{:S(2)}) %all-to-all-start.1) | async-done | bytes 524320 | tf_op jit(solution)/shard_map/all_to_all | solution.py:97
  43.0 6.7 %collective-permute-done = bf16[8,128,128]{2,1,0:T(8,128)(2,1)S(1)} collective-permute-done((bf16[8,128,128]{2,1,0:T(8,128)(2,1)S(1)}, bf16[8,128,128]{2,1,0:T(8,128)(2,1)S(1)}, u32[]{:S(2)}, u32[]{:S(2)}) %collective-permute-start) | collective-permute-done | bytes 262176 | tf_op jit(solution)/shard_map/ppermute | solution.py:135
  49.7 6.6 %collective-permute-done.1 = bf16[8,128,128]{2,1,0:T(8,128)(2,1)S(1)} collective-permute-done((bf16[8,128,128]{2,1,0:T(8,128)(2,1)S(1)}, bf16[8,128,128]{2,1,0:T(8,128)(2,1)S(1)}, u32[]{:S(2)}, u32[]{:S(2)}) %collective-permute-start.1) | collective-permute-done | bytes 262176 | tf_op jit(solution)/shard_map/ppermute | solution.py:135
  56.3 9.5 %collective-permute-done.2 = bf16[8,128,128]{2,1,0:T(8,128)(2,1)S(1)} collective-permute-done((bf16[8,128,128]{2,1,0:T(8,128)(2,1)S(1)}, bf16[8,128,128]{2,1,0:T(8,128)(2,1)S(1)}, u32[]{:S(2)}, u32[]{:S(2)}) %collective-permute-start.2) | collective-permute-done | bytes 262176 | tf_op jit(solution)/shard_map/ppermute | solution.py:135
  65.8 7.3 %collective-permute-done.3 = bf16[8,128,128]{2,1,0:T(8,128)(2,1)S(1)} collective-permute-done((bf16[8,128,128]{2,1,0:T(8,128)(2,1)S(1)}, bf16[8,128,128]{2,1,0:T(8,128)(2,1)S(1)}, u32[]{:S(2)}, u32[]{:S(2)}) %collective-permute-start.3) | collective-permute-done | bytes 262176 | tf_op jit(solution)/shard_map/ppermute | solution.py:135
  73.2 7.8 %collective-permute-done.4 = bf16[8,128,128]{2,1,0:T(8,128)(2,1)S(1)} collective-permute-done((bf16[8,128,128]{2,1,0:T(8,128)(2,1)S(1)}, bf16[8,128,128]{2,1,0:T(8,128)(2,1)S(1)}, u32[]{:S(2)}, u32[]{:S(2)}) %collective-permute-start.4) | collective-permute-done | bytes 262176 | tf_op jit(solution)/shard_map/ppermute | solution.py:135
  80.9 6.7 %collective-permute-done.5 = bf16[8,128,128]{2,1,0:T(8,128)(2,1)S(1)} collective-permute-done((bf16[8,128,128]{2,1,0:T(8,128)(2,1)S(1)}, bf16[8,128,128]{2,1,0:T(8,128)(2,1)S(1)}, u32[]{:S(2)}, u32[]{:S(2)}) %collective-permute-start.5) | collective-permute-done | bytes 262176 | tf_op jit(solution)/shard_map/ppermute | solution.py:135
  87.7 6.7 %collective-permute-done.6 = bf16[8,128,128]{2,1,0:T(8,128)(2,1)S(1)} collective-permute-done((bf16[8,128,128]{2,1,0:T(8,128)(2,1)S(1)}, bf16[8,128,128]{2,1,0:T(8,128)(2,1)S(1)}, u32[]{:S(2)}, u32[]{:S(2)}) %collective-permute-start.6) | collective-permute-done | bytes 262176 | tf_op jit(solution)/shard_map/ppermute | solution.py:135
  95.2 1.5 constant_dynamic-slice_fusion.3
  96.8 12.0 %while.31 = (s32[]{:T(128)}, f32[256,64]{0,1:T(8,128)S(1)}, bf16[64,128,128]{2,1,0:T(8,128)(2,1)}, bf16[256,128]{1,0:T(8,128)(2,1)S(1)}, s32[]{:T(128)}, /*index=5*/s32[]{:T(128)}, s32[]{:T(128)}, s32[]{:T(128)}) while((s32[]{:T(128)}, f32[256,64]{0,1:T(8,128)S(1)}, bf16[64,128,128]{2,1,0:T(8,128)(2,1)}, bf16[256,128]{1,0:T(8,128)(2,1)S(1)}, ...), condition=%wide.region_9.11_spmd, body=%wide.region_6.10_spmd.sunk | while | flops 68155400 | bytes 2998411 | solution.py:116
  96.8 1.0 constant_dynamic-slice_fusion.6
  98.3 1.0 constant_dynamic-slice_fusion.6
  99.8 1.0 constant_dynamic-slice_fusion.6
  101.3 1.0 constant_dynamic-slice_fusion.6
  102.8 1.0 constant_dynamic-slice_fusion.6
  104.3 1.0 constant_dynamic-slice_fusion.6
  105.8 1.0 constant_dynamic-slice_fusion.6
  107.3 1.0 constant_dynamic-slice_fusion.6
  109.0 1.5 broadcast_in_dim.131
  110.5 27.8 %while.32 = (s32[]{:T(128)}, f32[256,128]{1,0:T(8,128)S(1)}, bf16[8192,128]{1,0:T(8,128)(2,1)}, f32[256,64]{0,1:T(8,128)S(1)}, bf16[64,128,128]{2,1,0:T(8,128)(2...) while((s32[]{:T(128)}, f32[256,128]{1,0:T(8,128)S(1)}, ...), condition=%wide.region_12.14_spmd.clone, body=%wide.region_11.13_spmd.clone.sunk | while | flops 203229184 | bytes 7274735 | solution.py:161
  110.5 1.0 constant_dynamic-slice_fusion.7
  111.8 1.0 convolution_dynamic-update-slice_fusion.2
  113.2 0.7 fusion.54
  113.9 1.0 constant_dynamic-slice_fusion.7
  115.3 1.0 convolution_dynamic-update-slice_fusion.2
  116.6 0.7 fusion.54
  117.4 1.0 constant_dynamic-slice_fusion.7
  118.8 1.0 convolution_dynamic-update-slice_fusion.2
  120.1 0.7 fusion.54
  120.9 1.0 constant_dynamic-slice_fusion.7
  122.3 1.0 convolution_dynamic-update-slice_fusion.2
  123.6 0.7 fusion.54
  124.4 1.0 constant_dynamic-slice_fusion.7
  125.7 1.0 convolution_dynamic-update-slice_fusion.2
  127.1 0.7 fusion.54
  127.9 1.0 constant_dynamic-slice_fusion.7
  129.2 1.0 convolution_dynamic-update-slice_fusion.2
  130.6 0.7 fusion.54
  131.3 1.0 constant_dynamic-slice_fusion.7
  132.7 1.0 convolution_dynamic-update-slice_fusion.2
  134.0 0.7 fusion.54
  134.8 1.0 constant_dynamic-slice_fusion.7
  136.2 1.0 convolution_dynamic-update-slice_fusion.2
  137.5 0.7 fusion.54
  138.5 39.8 %reduce-scatter.5.cloned.1.call-done = bf16[1024,128]{1,0:T(8,128)(2,1)} async-done(((bf16[8192,128]{1,0:T(8,128)(2,1)}), bf16[1024,128]{1,0:T(8,128)(2,1)}) %reduce-scatter.5.cloned.1.call-update) | async-done | bytes 262160 | tf_op jit(solution)/shard_map/reduce_scatter | solution.py:165
  178.3 1.6 gather_fusion.1
  179.9 0.9 select_select_fusion.2
  180.8 4.6 %all-to-all-start.2 = ((bf16[4,4,128,128]{3,2,1,0:T(8,128)(2,1)}), bf16[4,4,128,128]{3,2,1,0:T(8,128)(2,1)S(1)}, u32[]{:S(2)}, u32[]{:S(2)}) async-start(bf16[4,4,128,128]{3,2,1,0:T(8,128)(2,1)} %select_select_fusion.2), calls=%async_computation.4 | async-start | bytes 1048576 | tf_op jit(solution)/shard_map/all_to_all | solution.py:170
  186.2 22.0 %reduce-scatter.3.cloned.1.call-done = bf16[64,128]{1,0:T(8,128)(2,1)} async-done(((bf16[256,128]{1,0:T(8,128)(2,1)}), bf16[64,128]{1,0:T(8,128)(2,1)}) %reduce-scatter.3.cloned.1.call-update) | async-done | bytes 16400 | tf_op jit(solution)/shard_map/reduce_scatter | solution.py:162
  208.2 1.3 convert_element_type.66
  209.6 0.6 gather_fusion.3
  210.4 0.7 fusion.8
  211.0 2.9 %convolution_convert_fusion = bf16[2048,1024]{1,0:T(8,128)(2,1)} fusion(bf16[1024,128]{1,0:T(8,128)(2,1)S(1)} %copy-done, bf16[2048,128]{1,0:T(8,128)(2,1)S(1)} %bitcast.129, f32[2048,128]{1,0:T(8,128)S(1)} %copy-done.2, f32[2048]{0:T(1024)S(1)} %fusion.8, f32[2048]{0:T(1024)S(1)} %add_rsqrt_fusion), kind=kOutput, calls=%fused_computation.25 | convolution fusion | flops 540540928 | bytes 6045696 | tf_op jit(solution)/shard_map/rd,hd->rh/dot_general | solution.py:176
  (129 shorter events, 13.8 us)
Async XLA Ops:
  7.2 9.5 %copy-start = (bf16[1024,128]{1,0:T(8,128)(2,1)S(1)}, bf16[1024,128]{1,0:T(8,128)(2,1)}, u32[]{:S(2)}) copy-start(bf16[1024,128]{1,0:T(8,128)(2,1)} %param.14) | copy-start | bytes 786436
  10.3 12.8 %all-to-all-start = ((s32[4,1,4]{2,1,0:T(1,128)}), s32[4,1,4]{2,1,0:T(1,128)S(1)}, u32[]{:S(2)}, u32[]{:S(2)}) async-start(s32[4,1,4]{2,1,0:T(1,128)} %bitcast.9), calls=%async_computation | async-start | bytes 4096 | tf_op jit(solution)/shard_map/all_to_all | solution.py:98
  20.2 1.0 copy-start.1
  20.2 67.4 %copy-start.5 = (s32[8,1,64]{2,1,0:T(1,128)S(1)}, s32[8,1,64]{2,1,0:T(1,128)}, u32[]{:S(2)}) copy-start(s32[8,1,64]{2,1,0:T(1,128)} %param.15) | copy-start | bytes 6148
  20.2 67.4 %copy-start.6 = (s32[8,1,64]{2,1,0:T(1,128)S(1)}, s32[8,1,64]{2,1,0:T(1,128)}, u32[]{:S(2)}) copy-start(s32[8,1,64]{2,1,0:T(1,128)} %param.16) | copy-start | bytes 6148
  23.1 19.0 %all-to-all-start.1 = ((bf16[4,4,128,128]{3,2,1,0:T(8,128)(2,1)}), bf16[4,4,128,128]{3,2,1,0:T(8,128)(2,1)S(1)}, u32[]{:S(2)}, u32[]{:S(2)}) async-start(bf16[4,4,128,128]{3,2,1,0:T(8,128)(2,1)} %bitcast.12), calls=%async_computation.1 | async-start | bytes 1048576 | tf_op jit(solution)/shard_map/all_to_all | solution.py:97
  28.2 68.5 %all-gather.2.cloned.1.call-start = ((), (), s32[]{:S(2)}) async-start(), calls=%async_computation.5 | async-start | bytes 2359296 | tf_op jit(solution)/shard_map/all_gather | solution.py:107
  42.9 6.8 %copy-start.4 = (bf16[8,128,128]{2,1,0:T(8,128)(2,1)}, bf16[8,128,128]{2,1,0:T(8,128)(2,1)S(1)}, u32[]{:S(2)}) copy-start(bf16[8,128,128]{2,1,0:T(8,128)(2,1)S(1)} %broadcast_select_fusion) | copy-start | bytes 786436
  42.9 6.7 %collective-permute-start = (bf16[8,128,128]{2,1,0:T(8,128)(2,1)S(1)}, bf16[8,128,128]{2,1,0:T(8,128)(2,1)S(1)}, u32[]{:S(2)}, u32[]{:S(2)}) collective-permute-start(bf16[8,128,128]{2,1,0:T(8,128)(2,1)S(1)} %broadcast_select_fusion), channel_id=1, source_target_pairs={{0,4},{4,8},{8,12},{12,16},{16,20},{20,24},{24,28},{28,0},{1,5},{5... | collective-permute-start | bytes 786440 | tf_op jit(solution)/shard_map/ppermute | solution.py:135
  49.6 6.7 %collective-permute-start.1 = (bf16[8,128,128]{2,1,0:T(8,128)(2,1)S(1)}, bf16[8,128,128]{2,1,0:T(8,128)(2,1)S(1)}, u32[]{:S(2)}, u32[]{:S(2)}) collective-permute-start(bf16[8,128,128]{2,1,0:T(8,128)(2,1)S(1)} %collective-permute-done), channel_id=1, source_target_pairs={{0,4},{4,8},{8,12},{12,16},{16,20},{20,24},{24,28},{28,0},{1,5},{5... | collective-permute-start | bytes 786440 | tf_op jit(solution)/shard_map/ppermute | solution.py:135
  49.7 128.6 %reduce-scatter.5.cloned.1.call-start = ((), (), s32[]{:S(2)}) async-start(), calls=%async_computation.7 | async-start | bytes 2359296 | tf_op jit(solution)/shard_map/reduce_scatter | solution.py:165
  56.3 9.5 %collective-permute-start.2 = (bf16[8,128,128]{2,1,0:T(8,128)(2,1)S(1)}, bf16[8,128,128]{2,1,0:T(8,128)(2,1)S(1)}, u32[]{:S(2)}, u32[]{:S(2)}) collective-permute-start(bf16[8,128,128]{2,1,0:T(8,128)(2,1)S(1)} %collective-permute-done.1), channel_id=1, source_target_pairs={{0,4},{4,8},{8,12},{12,16},{16,20},{20,24},{24,28},{28,0},{1,5},{5... | collective-permute-start | bytes 786440 | tf_op jit(solution)/shard_map/ppermute | solution.py:135
  65.8 7.3 %collective-permute-start.3 = (bf16[8,128,128]{2,1,0:T(8,128)(2,1)S(1)}, bf16[8,128,128]{2,1,0:T(8,128)(2,1)S(1)}, u32[]{:S(2)}, u32[]{:S(2)}) collective-permute-start(bf16[8,128,128]{2,1,0:T(8,128)(2,1)S(1)} %collective-permute-done.2), channel_id=1, source_target_pairs={{0,4},{4,8},{8,12},{12,16},{16,20},{20,24},{24,28},{28,0},{1,5},{5... | collective-permute-start | bytes 786440 | tf_op jit(solution)/shard_map/ppermute | solution.py:135
  73.2 7.8 %collective-permute-start.4 = (bf16[8,128,128]{2,1,0:T(8,128)(2,1)S(1)}, bf16[8,128,128]{2,1,0:T(8,128)(2,1)S(1)}, u32[]{:S(2)}, u32[]{:S(2)}) collective-permute-start(bf16[8,128,128]{2,1,0:T(8,128)(2,1)S(1)} %collective-permute-done.3), channel_id=1, source_target_pairs={{0,4},{4,8},{8,12},{12,16},{16,20},{20,24},{24,28},{28,0},{1,5},{5... | collective-permute-start | bytes 786440 | tf_op jit(solution)/shard_map/ppermute | solution.py:135
  80.9 6.7 %collective-permute-start.5 = (bf16[8,128,128]{2,1,0:T(8,128)(2,1)S(1)}, bf16[8,128,128]{2,1,0:T(8,128)(2,1)S(1)}, u32[]{:S(2)}, u32[]{:S(2)}) collective-permute-start(bf16[8,128,128]{2,1,0:T(8,128)(2,1)S(1)} %collective-permute-done.4), channel_id=1, source_target_pairs={{0,4},{4,8},{8,12},{12,16},{16,20},{20,24},{24,28},{28,0},{1,5},{5... | collective-permute-start | bytes 786440 | tf_op jit(solution)/shard_map/ppermute | solution.py:135
  87.6 6.7 %collective-permute-start.6 = (bf16[8,128,128]{2,1,0:T(8,128)(2,1)S(1)}, bf16[8,128,128]{2,1,0:T(8,128)(2,1)S(1)}, u32[]{:S(2)}, u32[]{:S(2)}) collective-permute-start(bf16[8,128,128]{2,1,0:T(8,128)(2,1)S(1)} %collective-permute-done.5), channel_id=1, source_target_pairs={{0,4},{4,8},{8,12},{12,16},{16,20},{20,24},{24,28},{28,0},{1,5},{5... | collective-permute-start | bytes 786440 | tf_op jit(solution)/shard_map/ppermute | solution.py:135
  94.8 2.0 copy-start.3
  138.3 47.9 %copy-start.7 = (s32[1,16]{1,0:T(1,128)S(1)}, s32[1,16]{1,0:T(1,128)}, u32[]{:S(2)}) copy-start(s32[1,16]{1,0:T(1,128)} %param.17) | copy-start | bytes 196
  138.3 72.1 %copy-start.2 = (f32[2048,128]{1,0:T(8,128)S(1)}, f32[2048,128]{1,0:T(8,128)}, u32[]{:S(2)}) copy-start(f32[2048,128]{1,0:T(8,128)} %copy-done.1) | copy-start | bytes 3145732
  180.8 28.8 %all-to-all-start.2 = ((bf16[4,4,128,128]{3,2,1,0:T(8,128)(2,1)}), bf16[4,4,128,128]{3,2,1,0:T(8,128)(2,1)S(1)}, u32[]{:S(2)}, u32[]{:S(2)}) async-start(bf16[4,4,128,128]{3,2,1,0:T(8,128)(2,1)} %select_select_fusion.2), calls=%async_computation.4 | async-start | bytes 1048576 | tf_op jit(solution)/shard_map/all_to_all | solution.py:170
  185.4 22.8 %reduce-scatter.3.cloned.1.call-start = ((), (), s32[]{:S(2)}) async-start(), calls=%async_computation.6 | async-start | bytes 81920 | tf_op jit(solution)/shard_map/reduce_scatter | solution.py:162
Sparse Core Ops, SparseCore 0:
  49.8 30.4 all-gather.1
  138.5 39.7 reduce-scatter.4
  188.4 19.7 reduce-scatter.2
